TPU v7x, 512 devices: a whole 4x8x8 slice. The times are simulated.
512 devices in a mesh: head: 8 (over z), tok: 64 (over x, y, core).
Axes of the slice: x: 4, y: 8, z: 8, core: 2. Of those that a mesh axis runs over, the one named last changes fastest.
Arguments:
- patches: bfloat16 [32768, 1280], P('tok')
- row_table: bfloat16 [64, 1280], replicated, may hold values from -0.59765625 to 0.59765625
- col_table: bfloat16 [64, 1280], replicated, may hold values from -0.59765625 to 0.59765625
- qkv_weight: bfloat16 [3, 1280, 1280], P(None, 'head'), may hold values from -0.15625 to 0.15625
- out_weight: bfloat16 [1280, 1280], P('head'), may hold values from -0.15625 to 0.15625
- merge_weight: bfloat16 [1280, 5120], P('head'), may hold values from -0.078125 to 0.078125
- segment_ids: int32 [32768], P('tok'), may hold values from 0 to 63, as said below
- image_grids: int32 [64, 2], replicated, may hold values from 2 to 62, as said below
- image_offsets: int32 [64], replicated, may hold values from 0 to 32736, as said below
- owners: int32 [64], replicated, may hold values from 0 to 63, each once
Outputs:
- delivered: bfloat16 [15872, 1280], P('tok', 'head')
Inputs may be any that keep to these rules, and one draw needn't show every extreme that they name: `segment_ids`: tokens of each image are consecutive and images follow in order; the pair p of token blocks (tokens 2 * p * 512 to 2 * (p + 1) * 512 - 1) holds exactly images 2 * p and 2 * p + 1, with no padding. `image_grids`: heights are even, widths are 16, and height times width is the image's token count. Within an image each 2x2 window of patches is four consecutive tokens (top left, top right, bottom left, bottom right), windows in row-major order. The longest image has exactly 992 tokens. `image_offsets`: the first token of each image, consistent with segment_ids. `owners`: every device index along tok owns exactly one image.
All inputs are finite; a program needn't handle non-finite values.
Results may differ from a plain program's by a relative error of at most 0.019.
Values may be sent and summed in bfloat16 or wider, within the bound.
No kernel may reach another device: no remote copies, remote signals or barrier semaphores. Data moves between devices by JAX's collectives and lax.ppermute only.
A program may use at most 64 MiB of HBM per device.

v0:
```python
import math
import jax
import jax.numpy as jnp
from jax import lax
from jax.sharding import PartitionSpec as P

HEAD_DIM = 80
CAP = 248


def partner(x, axis, apart):
    return lax.ppermute(x, axis, [(i, i ^ 1 << apart) for i in range(lax.axis_size(axis))])


def layer_norm(values):
    centered = values - jnp.mean(values, axis=-1, keepdims=True)
    variance = jnp.mean(centered * centered, axis=-1, keepdims=True)
    return centered * lax.rsqrt(variance + 1e-06)


def grid_place(token_pos, start_tok, width_now):
    local_pos = token_pos - start_tok
    window = local_pos // 4
    quarter = local_pos % 4
    half_width = jnp.maximum(width_now // 2, 1)
    row_index = 2 * (window // half_width) + quarter // 2
    col_index = 2 * (window % half_width) + quarter % 2
    return (row_index, col_index)


def dot_last(left, right):
    return lax.dot_general(
        left, right, (((1,), (1,)), ((), ())), preferred_element_type=jnp.float32
    )


def on_device(
    patches,
    row_table,
    col_table,
    qkv_weight,
    out_weight,
    merge_weight,
    segment_ids,
    image_grids,
    image_offsets,
    owners,
):
    block_rows = patches.shape[0]
    width_here = qkv_weight.shape[1]
    heads_here = width_here // HEAD_DIM
    image_count = owners.shape[0]
    image_ids = jnp.arange(image_count, dtype=jnp.int32)
    token_pos = lax.axis_index("tok") * block_rows + jnp.arange(block_rows, dtype=jnp.int32)
    member = segment_ids[:, None] == image_ids[None, :]
    start_tok = jnp.sum(jnp.where(member, image_offsets[None, :], 0), axis=1)
    width_now = jnp.sum(jnp.where(member, image_grids[None, :, 1], 0), axis=1)
    row_index, col_index = grid_place(token_pos, start_tok, width_now)
    side_ids = jnp.arange(row_table.shape[0], dtype=jnp.int32)
    row_onehot = (row_index[:, None] == side_ids[None, :]).astype(jnp.bfloat16)
    col_onehot = (col_index[:, None] == side_ids[None, :]).astype(jnp.bfloat16)
    resid = (
        patches.astype(jnp.float32)
        + jnp.dot(row_onehot, row_table, preferred_element_type=jnp.float32)
        + jnp.dot(col_onehot, col_table, preferred_element_type=jnp.float32)
    )
    normed = layer_norm(resid).astype(jnp.bfloat16)
    query_rows = dot_last(normed, qkv_weight[0]).astype(jnp.bfloat16)
    key_rows = dot_last(normed, qkv_weight[1]).astype(jnp.bfloat16)
    value_rows = dot_last(normed, qkv_weight[2]).astype(jnp.bfloat16)
    seg_wire = segment_ids.astype(jnp.bfloat16)
    far_keys, far_values, far_seg = partner((key_rows, value_rows, seg_wire), "tok", 0)
    query_heads = query_rows.reshape(block_rows, heads_here, HEAD_DIM)
    key_heads = jnp.concatenate([key_rows, far_keys], axis=0).reshape(
        2 * block_rows, heads_here, HEAD_DIM
    )
    value_heads = jnp.concatenate([value_rows, far_values], axis=0).reshape(
        2 * block_rows, heads_here, HEAD_DIM
    )
    query_seg = seg_wire.astype(jnp.float32)
    key_seg = jnp.concatenate([seg_wire, far_seg], axis=0).astype(jnp.float32)
    scores = jnp.einsum(
        "qhd,khd->hqk", query_heads, key_heads, preferred_element_type=jnp.float32
    ) * (1.0 / math.sqrt(HEAD_DIM))
    same_image = query_seg[:, None] == key_seg[None, :]
    raw_weights = jnp.where(same_image[None], jnp.exp(scores), 0.0)
    weight_sum = jnp.sum(raw_weights, axis=-1, keepdims=True)
    attn_probs = (raw_weights / weight_sum).astype(jnp.bfloat16)
    mixed = jnp.einsum("hqk,khd->qhd", attn_probs, value_heads, preferred_element_type=jnp.float32)
    attended = mixed.reshape(block_rows, width_here).astype(jnp.bfloat16)
    partial_sum = jnp.dot(attended, out_weight, preferred_element_type=jnp.float32)
    head_total = lax.psum(partial_sum.astype(jnp.bfloat16), "head").astype(jnp.float32)
    normed_two = layer_norm(resid + head_total).astype(jnp.bfloat16)
    merged = normed_two.reshape(block_rows // 4, 4 * normed_two.shape[1])
    projected = dot_last(merged, merge_weight).astype(jnp.bfloat16)
    owner_mask = owners == lax.axis_index("tok")
    image_id = jnp.sum(jnp.where(owner_mask, image_ids, 0))
    chosen = image_ids == image_id
    first_row = jnp.sum(jnp.where(chosen, image_offsets, 0)) // 4
    merged_count = jnp.sum(jnp.where(chosen, image_grids[:, 0] * image_grids[:, 1], 0)) // 4
    slot_ids = jnp.arange(CAP, dtype=jnp.int32)
    piece_rows = lax.all_gather(projected, "tok", axis=0, tiled=True)
    row_ids = jnp.arange(piece_rows.shape[0], dtype=jnp.int32)
    slot_of = row_ids - first_row
    inside = row_ids < first_row + merged_count
    selector = (slot_of[None, :] == slot_ids[:, None]) & inside[None, :]
    owner_rows = jnp.dot(
        selector.astype(jnp.bfloat16), piece_rows, preferred_element_type=jnp.float32
    )
    return owner_rows.astype(jnp.bfloat16)


def solution(mesh):
    placed = (
        P("tok", None),
        P(),
        P(),
        P(None, "head", None),
        P("head", None),
        P("head", None),
        P("tok"),
        P(),
        P(),
        P(),
    )
    return jax.shard_map(
        on_device, mesh=mesh, in_specs=placed, out_specs=P("tok", "head"), check_vma=False
    )
```

profile of v0, /device:TPU:1, one launch (start us, length us, event | category | flops | bytes accessed | tf_op | source)
XLA Modules:
  0.0 213.2 jit_solution(1868882156168978352)
XLA Ops:
  6.5 0.0 copy-start
  6.5 0.0 copy-start.5
  6.5 0.0 all-reduce.2.cloned.1.call-start
  6.5 0.8 slice_bitcast_fusion
  7.4 0.8 select_reduce_fusion
  8.1 0.1 fusion.25
  8.3 2.0 convolution_add_fusion.1
  10.3 0.0 copy-done.5
  10.3 0.6 fusion.36
  10.9 0.0 copy-start.1
  10.9 0.4 multiply_reduce_fusion.1
  11.3 0.0 copy-start.9
  11.4 0.0 copy-start.6
  11.4 0.3 multiply_convert_fusion.1
  11.7 0.7 copy-done.1
  12.4 0.7 copy-done.9
  13.1 0.6 convolution_convert_fusion.3
  13.7 8.8 %collective-permute-start = (bf16[512,160]{0,1:T(8,128)(2,1)S(1)}, bf16[512,160]{0,1:T(8,128)(2,1)S(1)}, u32[]{:S(2)}, u32[]{:S(2)}) collective-permute-start(bf16[512,160]{0,1:T(8,128)(2,1)S(1)} %convolution_convert_fusion.3), channel_id=1, source_target_pairs={{0,1},{1,0},{2,3},{3,2},{4,5},{5,4},{6,7},{7,6},{8,9},{9,8},{10,11... | collective-permute-start | bytes 491528 | tf_op jit(solution)/shard_map/ppermute | solution.py:12
  22.5 0.0 copy-done.6
  22.5 1.9 collective-permute-start.1
  24.5 0.6 convolution_convert_fusion.1
  25.0 2.4 %collective-permute-start.2 = (bf16[512,160]{0,1:T(8,128)(2,1)S(1)}, bf16[512,160]{0,1:T(8,128)(2,1)S(1)}, u32[]{:S(2)}, u32[]{:S(2)}) collective-permute-start(bf16[512,160]{0,1:T(8,128)(2,1)S(1)} %convolution_convert_fusion.1), channel_id=1, source_target_pairs={{0,1},{1,0},{2,3},{3,2},{4,5},{5,4},{6,7},{7,6},{8,9},{9,8},{10,11... | collective-permute-start | bytes 491528 | tf_op jit(solution)/shard_map/ppermute | solution.py:12
  27.5 0.6 convolution_convert_fusion.2
  28.0 0.0 collective-permute-done.1
  28.1 0.4 broadcast_compare_fusion
  28.4 0.0 collective-permute-done.2
  28.5 1.5 fusion.5
  30.0 0.0 collective-permute-done
  30.0 0.0 copy-start.4
  30.0 1.4 fusion.7
  31.4 0.0 copy-done.4
  31.4 1.6 convolution_convert_fusion
  33.0 0.0 all-reduce.2.cloned.1.call-update
  33.1 0.0 all-gather.2.cloned.1.call-start
  33.1 78.2 %all-reduce.2.cloned.1.call-done = bf16[512,1280]{1,0:T(8,128)(2,1)} async-done(((bf16[512,1280]{1,0:T(8,128)(2,1)}), bf16[512,1280]{1,0:T(8,128)(2,1)}) %all-reduce.2.cloned.1.call-update) | async-done | bytes 1310736 | tf_op jit(solution)/shard_map/psum | solution.py:92
  111.4 0.0 copy-start.2
  111.4 0.0 copy-start.3
  111.4 2.6 %fusion.11 = f32[512]{0:T(512)S(1)} fusion(f32[512,1280]{1,0:T(8,128)} %copy-done.1, bf16[512,1280]{1,0:T(8,128)(2,1)} %all-reduce.2.cloned.1.call-done), kind=kLoop, calls=%fused_computation.24 | loop fusion | flops 1965568 | bytes 3934208 | tf_op jit(solution)/shard_map/reduce_sum | solution.py:16
  114.0 0.3 copy-done.2
  114.3 0.4 copy-done.3
  114.6 0.5 multiply_reduce_fusion
  115.2 1.5 multiply_convert_fusion
  116.7 0.0 copy-start.10
  116.7 0.0 copy-start.7
  116.7 0.0 copy-start.8
  116.7 2.5 %reshape.198 = bf16[128,5120]{1,0:T(8,128)(2,1)S(1)} reshape(bf16[512,1280]{1,0:T(8,128)(2,1)} %multiply_convert_fusion) | data formatting | bytes 2621440 | tf_op jit(solution)/shard_map/reshape | solution.py:94
  119.2 0.0 copy-done
  119.2 1.2 convolution_convert_fusion.4
  120.4 0.0 all-gather.2.cloned.1.call-update
  120.5 0.0 copy-done.10
  120.5 0.6 fusion.32
  121.1 0.0 copy-done.7
  121.1 0.0 copy-done.8
  121.1 1.3 fusion.30
  127.3 74.8 %all-gather.2.cloned.1.call-done = bf16[8192,160]{0,1:T(8,128)(2,1)} async-done(((bf16[128,160]{0,1:T(8,128)(2,1)}), bf16[8192,160]{0,1:T(8,128)(2,1)}) %all-gather.2.cloned.1.call-update) | async-done | bytes 2621456 | tf_op jit(solution)/shard_map/all_gather | solution.py:102
  202.1 4.3 %fusion.8 = bf16[248,160]{0,1:T(8,128)(2,1)} fusion(bf16[8192,160]{0,1:T(8,128)(2,1)} %all-gather.2.cloned.1.call-done, s32[8192]{0:T(1024)S(1)} %iota_subtract_fusion, pred[8192]{0:T(1024)(128)(4,1)S(1)} %iota_compare_fusion.6), kind=kOutput, calls=%fused_computation.21 | convolution fusion | flops 654220032 | bytes 2741760 | tf_op jit(solution)/shard_map/dot_general | solution.py:107
  (10 shorter events, 0.1 us)
Async XLA Ops:
  6.5 112.7 %copy-start = (bf16[160,5120]{1,0:T(8,128)(2,1)S(1)}, bf16[160,5120]{1,0:T(8,128)(2,1)}, u32[]{:S(2)}) copy-start(bf16[160,5120]{1,0:T(8,128)(2,1)} %param.15) | copy-start | bytes 4915204
  6.5 3.7 %copy-start.5 = (bf16[64,1280]{1,0:T(8,128)(2,1)S(1)}, bf16[64,1280]{1,0:T(8,128)(2,1)}, u32[]{:S(2)}) copy-start(bf16[64,1280]{1,0:T(8,128)(2,1)} %param.12) | copy-start | bytes 491524
  6.5 104.8 %all-reduce.2.cloned.1.call-start = ((), (), s32[]{:S(2)}) async-start(), calls=%async_computation | async-start | bytes 2621440 | tf_op jit(solution)/shard_map/psum | solution.py:92
  10.9 1.5 copy-start.1
  11.3 1.8 copy-start.9
  11.4 11.2 %copy-start.6 = (s32[512]{0:T(512)S(1)}, s32[512]{0:T(512)}, u32[]{:S(2)}) copy-start(s32[512]{0:T(512)} %param.16) | copy-start | bytes 6148
  13.7 16.3 %collective-permute-start = (bf16[512,160]{0,1:T(8,128)(2,1)S(1)}, bf16[512,160]{0,1:T(8,128)(2,1)S(1)}, u32[]{:S(2)}, u32[]{:S(2)}) collective-permute-start(bf16[512,160]{0,1:T(8,128)(2,1)S(1)} %convolution_convert_fusion.3), channel_id=1, source_target_pairs={{0,1},{1,0},{2,3},{3,2},{4,5},{5,4},{6,7},{7,6},{8,9},{9,8},{10,11... | collective-permute-start | bytes 491528 | tf_op jit(solution)/shard_map/ppermute | solution.py:12
  22.5 5.5 %collective-permute-start.1 = (bf16[512]{0:T(512)(128)(2,1)S(1)}, bf16[512]{0:T(512)(128)(2,1)S(1)}, u32[]{:S(2)}, u32[]{:S(2)}) collective-permute-start(bf16[512]{0:T(512)(128)(2,1)S(1)} %get-tuple-element.8), channel_id=1, source_target_pairs={{0,1},{1,0},{2,3},{3,2},{4,5},{5,4},{6,7},{7,6},{8,9},{9,8},{10,11... | collective-permute-start | bytes 3080 | tf_op jit(solution)/shard_map/ppermute | solution.py:12
  25.0 3.4 %collective-permute-start.2 = (bf16[512,160]{0,1:T(8,128)(2,1)S(1)}, bf16[512,160]{0,1:T(8,128)(2,1)S(1)}, u32[]{:S(2)}, u32[]{:S(2)}) collective-permute-start(bf16[512,160]{0,1:T(8,128)(2,1)S(1)} %convolution_convert_fusion.1), channel_id=1, source_target_pairs={{0,1},{1,0},{2,3},{3,2},{4,5},{5,4},{6,7},{7,6},{8,9},{9,8},{10,11... | collective-permute-start | bytes 491528 | tf_op jit(solution)/shard_map/ppermute | solution.py:12
  30.0 1.4 copy-start.4
  33.1 169.0 %all-gather.2.cloned.1.call-start = ((), (), s32[]{:S(2)}) async-start(), calls=%async_computation.1 | async-start | bytes 2662400 | tf_op jit(solution)/shard_map/all_gather | solution.py:102
  111.4 2.9 %copy-start.2 = (f32[512,1280]{1,0:T(8,128)S(1)}, f32[512,1280]{1,0:T(8,128)}, u32[]{:S(2)}) copy-start(f32[512,1280]{1,0:T(8,128)} %copy-done.1) | copy-start | bytes 7864324
  111.4 3.3 %copy-start.3 = (bf16[512,1280]{1,0:T(8,128)(2,1)S(1)}, bf16[512,1280]{1,0:T(8,128)(2,1)}, u32[]{:S(2)}) copy-start(bf16[512,1280]{1,0:T(8,128)(2,1)} %all-reduce.2.cloned.1.call-done) | copy-start | bytes 3932164
  116.7 3.8 %copy-start.10 = (s32[64]{0:T(128)S(1)}, s32[64]{0:T(128)}, u32[]{:S(2)}) copy-start(s32[64]{0:T(128)} %param.19) | copy-start | bytes 772
  116.7 4.4 %copy-start.7 = (s32[64]{0:T(128)S(1)}, s32[64]{0:T(128)}, u32[]{:S(2)}) copy-start(s32[64]{0:T(128)} %param.18) | copy-start | bytes 772
  116.7 4.4 %copy-start.8 = (s32[64,2]{0,1:T(2,128)S(1)}, s32[64,2]{0,1:T(2,128)}, u32[]{:S(2)}) copy-start(s32[64,2]{0,1:T(2,128)} %param.17) | copy-start | bytes 1540
Sparse Core Ops, SparseCore 0:
  33.2 78.1 all-reduce.1
  120.6 81.4 all-gather.1
where the time goes:
time: 214 us; the launch traced here: 213 us
  waiting for transfers between devices  153 us (71%)
  between operations  18.4 us (9%)
  matrix products  14.4 us (7%)
  starting transfers between devices  13.2 us (6%)
  other arithmetic  8.66 us (4%)
  local copies, waits for them, and re-layouts  5.5 us (3%)
    psum x1, waiting for transfers between devices, on_device(): lax.psum(partial_sum.astype(jnp.bfloat16), 'head').astype(jnp.float32)  78.2 us
    all_gather x1, waiting for transfers between devices, on_device(): piece_rows = lax.all_gather(projected, 'tok', axis=0, tiled=True)  74.8 us
    ppermute x3, starting transfers between devices, partner(): lax.ppermute(x, axis, [(i, i ^ 1 << apart) for i in range(lax.axis_size(a...  13.1 us
    dot_general x1, matrix products, on_device(): jnp.dot(selector.astype(jnp.bfloat16), piece_rows, preferred_element_type...  4.35 us
  transfers between devices with their start and end apart: 5, of which 2 were waited for; matrix products, arithmetic and copies ran while one was open for 2% of the time, Pallas kernels for 0%

commit v1 on v0

--- a/solution.py
+++ b/solution.py
@@ -1,3 +1,4 @@
+import functools
 import math
 import jax
 import jax.numpy as jnp
@@ -6,6 +7,13 @@
 
 HEAD_DIM = 80
 CAP = 248
+
+
+def write_halves_on(work_x, named_axis):
+    return lax.all_gather(work_x, named_axis).sum(axis=0)
+
+
+lead_classes_all = functools.partial(write_halves_on, named_axis="head")
 
 
 def partner(x, axis, apart):
@@ -89,7 +97,7 @@
     mixed = jnp.einsum("hqk,khd->qhd", attn_probs, value_heads, preferred_element_type=jnp.float32)
     attended = mixed.reshape(block_rows, width_here).astype(jnp.bfloat16)
     partial_sum = jnp.dot(attended, out_weight, preferred_element_type=jnp.float32)
-    head_total = lax.psum(partial_sum.astype(jnp.bfloat16), "head").astype(jnp.float32)
+    head_total = lead_classes_all(partial_sum.astype(jnp.bfloat16)).astype(jnp.float32)
     normed_two = layer_norm(resid + head_total).astype(jnp.bfloat16)
     merged = normed_two.reshape(block_rows // 4, 4 * normed_two.shape[1])
     projected = dot_last(merged, merge_weight).astype(jnp.bfloat16)

time: 214 us -> 253 us (1.18)
  waiting for transfers between devices: 153 us -> 187 us
  other arithmetic: 8.66 us -> 14.6 us
    all_gather x0 -> x1, waiting for transfers between devices: none -> 116 us  [write_halves_on(): return lax.all_gather(work_x, named_axis).sum(axis=0)]
    psum x1 -> x0, waiting for transfers between devices: 78.2 us -> none  [on_device(): lax.psum(partial_sum.astype(jnp.bfloat16), 'head').astype(jnp.float32)]
    reduce_sum x0 -> x1, other arithmetic: none -> 6.23 us  [write_halves_on(): return lax.all_gather(work_x, named_axis).sum(axis=0)]
    all_gather x1, waiting for transfers between devices: 74.8 us -> 70.6 us  [on_device(): piece_rows = lax.all_gather(projected, 'tok', axis=0, tiled=True)]
where the time goes in v1:
time: 253 us; the launch traced here: 252 us
  waiting for transfers between devices  187 us (74%)
  between operations  18.5 us (7%)
  other arithmetic  14.6 us (6%)
  matrix products  14.4 us (6%)
  starting transfers between devices  13.3 us (5%)
  local copies, waits for them, and re-layouts  5.1 us (2%)
    all_gather x1, waiting for transfers between devices, write_halves_on(): return lax.all_gather(work_x, named_axis).sum(axis=0)  116 us
    all_gather x1, waiting for transfers between devices, on_device(): piece_rows = lax.all_gather(projected, 'tok', axis=0, tiled=True)  70.6 us
    ppermute x3, starting transfers between devices, partner(): lax.ppermute(x, axis, [(i, i ^ 1 << apart) for i in range(lax.axis_size(a...  13.1 us
    reduce_sum x1, other arithmetic, write_halves_on(): return lax.all_gather(work_x, named_axis).sum(axis=0)  6.23 us
  transfers between devices with their start and end apart: 5, of which 2 were waited for; matrix products, arithmetic and copies ran while one was open for 2% of the time, Pallas kernels for 0%

profile of v1, /device:TPU:1, one launch (start us, length us, event | category | flops | bytes accessed | tf_op | source)
XLA Modules:
  0.0 252.4 jit_solution(289164897657811070)
XLA Ops:
  6.5 0.0 copy-start
  6.5 0.0 copy-start.4
  6.5 0.0 all-gather.6.cloned.1.call-start
  6.5 0.8 slice_bitcast_fusion
  7.4 0.8 select_reduce_fusion
  8.1 0.1 fusion.25
  8.3 2.0 convolution_add_fusion.1
  10.3 0.0 copy-done.4
  10.3 0.6 fusion.36
  10.9 0.0 copy-start.1
  10.9 0.4 multiply_reduce_fusion.1
  11.3 0.0 copy-start.8
  11.4 0.0 copy-start.5
  11.4 0.3 multiply_convert_fusion.1
  11.7 0.8 copy-done.1
  12.4 0.7 copy-done.8
  13.1 0.6 convolution_convert_fusion.1
  13.7 8.8 %collective-permute-start.2 = (bf16[512,160]{0,1:T(8,128)(2,1)S(1)}, bf16[512,160]{0,1:T(8,128)(2,1)S(1)}, u32[]{:S(2)}, u32[]{:S(2)}) collective-permute-start(bf16[512,160]{0,1:T(8,128)(2,1)S(1)} %convolution_convert_fusion.1), channel_id=1, source_target_pairs={{0,1},{1,0},{2,3},{3,2},{4,5},{5,4},{6,7},{7,6},{8,9},{9,8},{10,11... | collective-permute-start | bytes 491528 | tf_op jit(solution)/shard_map/ppermute | solution.py:20
  22.5 0.0 copy-done.5
  22.5 1.9 collective-permute-start.1
  24.5 0.6 convolution_convert_fusion.3
  25.0 2.4 collective-permute-start
  27.5 0.6 convolution_convert_fusion.2
  28.0 0.0 collective-permute-done.1
  28.1 0.4 broadcast_compare_fusion
  28.4 0.0 collective-permute-done.2
  28.5 1.5 fusion.5
  29.9 0.0 collective-permute-done
  30.0 0.0 copy-start.3
  30.0 1.4 fusion.7
  31.4 0.0 copy-done.3
  31.4 1.6 convolution_convert_fusion
  33.0 0.0 all-gather.6.cloned.1.call-update
  33.0 0.2 all-gather.4.cloned.1.call-start
  33.3 115.9 %all-gather.6.cloned.1.call-done = bf16[4096,1280]{1,0:T(8,128)(2,1)} async-done(((bf16[512,1280]{1,0:T(8,128)(2,1)}), bf16[4096,1280]{1,0:T(8,128)(2,1)}) %all-gather.6.cloned.1.call-update) | async-done | bytes 10485776 | tf_op jit(solution)/shard_map/all_gather | solution.py:13
  149.2 6.2 %reduce_sum.110 = bf16[512,1280]{1,0:T(8,128)(2,1)S(1)} reduce(bf16[8,512,1280]{2,1,0:T(8,128)(2,1)} %bitcast.37, bf16[]{:T(256)} %constant.100.clone.1), dimensions={0}, to_apply=%region_8.9 | reduce | flops 4587520 | bytes 11796482 | tf_op jit(solution)/shard_map/reduce_sum | solution.py:13
  155.4 0.0 copy-start.2
  155.4 2.2 fusion.11
  157.7 0.3 copy-done.2
  157.9 0.6 multiply_reduce_fusion
  158.5 1.5 multiply_convert_fusion
  160.0 0.0 copy-start.9
  160.0 0.0 copy-start.6
  160.0 0.0 copy-start.7
  160.0 2.5 reshape.198
  162.6 0.0 copy-done
  162.6 1.2 convolution_convert_fusion.4
  163.8 0.0 all-gather.4.cloned.1.call-update
  163.8 0.0 copy-done.9
  163.8 0.6 fusion.32
  164.5 0.0 copy-done.6
  164.5 0.0 copy-done.7
  164.5 1.3 fusion.30
  170.6 70.6 %all-gather.4.cloned.1.call-done = bf16[8192,160]{0,1:T(8,128)(2,1)} async-done(((bf16[128,160]{0,1:T(8,128)(2,1)}), bf16[8192,160]{0,1:T(8,128)(2,1)}) %all-gather.4.cloned.1.call-update) | async-done | bytes 2621456 | tf_op jit(solution)/shard_map/all_gather | solution.py:110
  241.2 4.4 %fusion.8 = bf16[248,160]{0,1:T(8,128)(2,1)} fusion(bf16[8192,160]{0,1:T(8,128)(2,1)} %all-gather.4.cloned.1.call-done, s32[8192]{0:T(1024)S(1)} %iota_subtract_fusion, pred[8192]{0:T(1024)(128)(4,1)S(1)} %iota_compare_fusion.6), kind=kOutput, calls=%fused_computation.21 | convolution fusion | flops 654220032 | bytes 2741760 | tf_op jit(solution)/shard_map/dot_general | solution.py:115
  (10 shorter events, 0.1 us)
Async XLA Ops:
  6.5 156.0 %copy-start = (bf16[160,5120]{1,0:T(8,128)(2,1)S(1)}, bf16[160,5120]{1,0:T(8,128)(2,1)}, u32[]{:S(2)}) copy-start(bf16[160,5120]{1,0:T(8,128)(2,1)} %param.15) | copy-start | bytes 4915204
  6.5 3.7 %copy-start.4 = (bf16[64,1280]{1,0:T(8,128)(2,1)S(1)}, bf16[64,1280]{1,0:T(8,128)(2,1)}, u32[]{:S(2)}) copy-start(bf16[64,1280]{1,0:T(8,128)(2,1)} %param.12) | copy-start | bytes 491524
  6.5 142.6 %all-gather.6.cloned.1.call-start = ((), (), s32[]{:S(2)}) async-start(), calls=%async_computation.1 | async-start | bytes 11796480 | tf_op jit(solution)/shard_map/all_gather | solution.py:13
  10.9 1.5 copy-start.1
  11.3 1.8 copy-start.8
  11.4 11.2 %copy-start.5 = (s32[512]{0:T(512)S(1)}, s32[512]{0:T(512)}, u32[]{:S(2)}) copy-start(s32[512]{0:T(512)} %param.16) | copy-start | bytes 6148
  13.7 14.7 %collective-permute-start.2 = (bf16[512,160]{0,1:T(8,128)(2,1)S(1)}, bf16[512,160]{0,1:T(8,128)(2,1)S(1)}, u32[]{:S(2)}, u32[]{:S(2)}) collective-permute-start(bf16[512,160]{0,1:T(8,128)(2,1)S(1)} %convolution_convert_fusion.1), channel_id=1, source_target_pairs={{0,1},{1,0},{2,3},{3,2},{4,5},{5,4},{6,7},{7,6},{8,9},{9,8},{10,11... | collective-permute-start | bytes 491528 | tf_op jit(solution)/shard_map/ppermute | solution.py:20
  22.5 5.5 %collective-permute-start.1 = (bf16[512]{0:T(512)(128)(2,1)S(1)}, bf16[512]{0:T(512)(128)(2,1)S(1)}, u32[]{:S(2)}, u32[]{:S(2)}) collective-permute-start(bf16[512]{0:T(512)(128)(2,1)S(1)} %get-tuple-element.8), channel_id=1, source_target_pairs={{0,1},{1,0},{2,3},{3,2},{4,5},{5,4},{6,7},{7,6},{8,9},{9,8},{10,11... | collective-permute-start | bytes 3080 | tf_op jit(solution)/shard_map/ppermute | solution.py:20
  25.0 4.9 %collective-permute-start = (bf16[512,160]{0,1:T(8,128)(2,1)S(1)}, bf16[512,160]{0,1:T(8,128)(2,1)S(1)}, u32[]{:S(2)}, u32[]{:S(2)}) collective-permute-start(bf16[512,160]{0,1:T(8,128)(2,1)S(1)} %convolution_convert_fusion.3), channel_id=1, source_target_pairs={{0,1},{1,0},{2,3},{3,2},{4,5},{5,4},{6,7},{7,6},{8,9},{9,8},{10,11... | collective-permute-start | bytes 491528 | tf_op jit(solution)/shard_map/ppermute | solution.py:20
  30.0 1.4 copy-start.3
  33.0 208.2 %all-gather.4.cloned.1.call-start = ((), (), s32[]{:S(2)}) async-start(), calls=%async_computation | async-start | bytes 2662400 | tf_op jit(solution)/shard_map/all_gather | solution.py:110
  155.4 2.5 %copy-start.2 = (f32[512,1280]{1,0:T(8,128)S(1)}, f32[512,1280]{1,0:T(8,128)}, u32[]{:S(2)}) copy-start(f32[512,1280]{1,0:T(8,128)} %copy-done.1) | copy-start | bytes 7864324
  160.0 3.8 %copy-start.9 = (s32[64]{0:T(128)S(1)}, s32[64]{0:T(128)}, u32[]{:S(2)}) copy-start(s32[64]{0:T(128)} %param.19) | copy-start | bytes 772
  160.0 4.4 %copy-start.6 = (s32[64]{0:T(128)S(1)}, s32[64]{0:T(128)}, u32[]{:S(2)}) copy-start(s32[64]{0:T(128)} %param.18) | copy-start | bytes 772
  160.0 4.4 %copy-start.7 = (s32[64,2]{0,1:T(2,128)S(1)}, s32[64,2]{0,1:T(2,128)}, u32[]{:S(2)}) copy-start(s32[64,2]{0,1:T(2,128)} %param.17) | copy-start | bytes 1540
Sparse Core Ops, SparseCore 0:
  33.1 115.9 all-gather.5
  163.9 77.2 all-gather.3
